TPU v7x, 256 devices: a whole 4x4x8 slice. The times are simulated.
256 devices in a mesh: event: 8 (over x, z_lo), cuts: 32 (over z_hi, y, core).
Axes of the slice: x: 4, y: 4, z: 8 (z_hi: 4, z_lo: 2; z = z_hi * 2 + z_lo), core: 2. Of those that a mesh axis runs over, the one named last changes fastest.
Arguments:
- forward_displacement: float32 [8, 557568], P('event', 'cuts'), may hold values from -6 to 6
- forward_velocity: float32 [8, 557568], P('event', 'cuts'), may hold values from -6 to 6
- adjoint_displacement: float32 [8, 557568], P('event', 'cuts'), may hold values from -6 to 6
- adjoint_velocity: float32 [8, 557568], P('event', 'cuts'), may hold values from -6 to 6
- inverse_mass: float32 [557568], P('cuts'), may hold values from 0.3 to 3
- shear_modulus: float32 [125, 8192], P(None, 'cuts'), may hold values from 0.5 to 4
- connectivity: int32 [125, 8192], P(None, 'cuts'), may hold values from 0 to 18512, as said below
- face_points: int32 [32, 1152], P('cuts'), may hold values from 0 to 1088, as said below
- element_count: int32 [32], P('cuts'), may hold values from 128 to 256, as said below
Outputs:
- forward_displacement_next: float32 [8, 557568], P('event', 'cuts')
- forward_velocity_next: float32 [8, 557568], P('event', 'cuts')
- adjoint_displacement_next: float32 [8, 557568], P('event', 'cuts')
- adjoint_velocity_next: float32 [8, 557568], P('event', 'cuts')
- shear_kernel: float32 [512, 1089], P('cuts')
Inputs may be any that keep to these rules, and one draw needn't show every extreme that they name: `connectivity`: slot n of slice s is the element (ex, ey, ez) of a structured block of 4 x 8 x 8 elements, in an order drawn per slice; its point (i, j, k) has coordinates x = 4 ex + i, y = 4 ey + j, z = 4 ez + k and index x 1089 + y * 33 + z for x < 16; points with x = 16 lie on the next slice's first plane and have index 17424 + g, where g is their slot in the next slice's face list. `face_points`: row s lists in slots 0 to 1088 each point of slice s with x = 0 once; slots 1089 to 1151 hold 0. `element_count`: some slice has all 256 slots live in every draw.
All inputs are finite; a program needn't handle non-finite values.
Results may differ from a plain program's by a relative error of at most 0.0001.
Values sent between devices are 32-bit elements; how exact they have to be, the bound alone decides.
A program may use at most 128 MiB of HBM per device.

v0:
```python
import jax
import jax.numpy as jnp
import numpy as np
from jax import lax
from jax.sharding import PartitionSpec as P

NGLL = 5
PXU = 16
PY = 33
PZ = 33
PYZ = 1089
NPTS = 17424
NBUF = 1152
time_step = 0.02
cross_sigma = 1.5
cross_reach = 4


def from_behind(block, axis, distance):
    devices = range(lax.axis_size(axis))
    route = [((i - distance) % len(devices), i) for i in devices]
    return lax.ppermute(block, axis, route)


def with_halo(cells, sides, width):
    for axis, dim in sides:
        count = lax.axis_size(axis)
        head = lax.slice_in_dim(cells, 0, width, axis=dim)
        tail = lax.slice_in_dim(cells, cells.shape[dim] - width, cells.shape[dim], axis=dim)
        cells = jnp.concatenate(
            [
                lax.ppermute(tail, axis, [(i, (i + 1) % count) for i in range(count)]),
                cells,
                lax.ppermute(head, axis, [((i + 1) % count, i) for i in range(count)]),
            ],
            axis=dim,
        )
    return cells


def gll_tables():
    nodes = np.array([-1.0, -np.sqrt(3.0 / 7.0), 0.0, np.sqrt(3.0 / 7.0), 1.0])
    quad_weights = np.array([0.1, 49.0 / 90.0, 32.0 / 45.0, 49.0 / 90.0, 0.1])
    barycentric = np.array(
        [
            1.0
            / np.prod(
                [
                    nodes[node_row] - nodes[node_column]
                    for node_column in range(5)
                    if node_column != node_row
                ]
            )
            for node_row in range(5)
        ]
    )
    derivative = np.zeros((5, 5))
    for node_row in range(5):
        for node_column in range(5):
            if node_column != node_row:
                derivative[node_row, node_column] = (
                    barycentric[node_column]
                    / barycentric[node_row]
                    / (nodes[node_row] - nodes[node_column])
                )
        derivative[node_row, node_row] = -np.sum(derivative[node_row])
    weights_cube = (
        quad_weights[:, None, None] * quad_weights[None, :, None] * quad_weights[None, None, :]
    ).reshape(125)
    return (
        jnp.asarray(derivative, dtype=jnp.float32),
        jnp.asarray(weights_cube, dtype=jnp.float32),
    )


def gradients(cube, derivative):
    grad_x = jnp.einsum("il,ljkn->ijkn", derivative, cube, precision=lax.Precision.HIGHEST)
    grad_y = jnp.einsum("jl,ilkn->ijkn", derivative, cube, precision=lax.Precision.HIGHEST)
    grad_z = jnp.einsum("kl,ijln->ijkn", derivative, cube, precision=lax.Precision.HIGHEST)
    return (grad_x, grad_y, grad_z)


def stiffness(grads, flux_cube, derivative):
    term_x = jnp.einsum(
        "li,ljkn->ijkn", derivative, flux_cube * grads[0], precision=lax.Precision.HIGHEST
    )
    term_y = jnp.einsum(
        "lj,ilkn->ijkn", derivative, flux_cube * grads[1], precision=lax.Precision.HIGHEST
    )
    term_z = jnp.einsum(
        "lk,ijln->ijkn", derivative, flux_cube * grads[2], precision=lax.Precision.HIGHEST
    )
    return -(term_x + term_y + term_z)


def along_weight(offset):
    sigma = PXU / 4.0
    return jnp.exp(-offset * offset / (2.0 * sigma * sigma))


def along_band():
    offsets = jnp.arange(-PXU, PXU + 1, dtype=jnp.int32).astype(jnp.float32)
    norm_total = jnp.sum(along_weight(offsets))
    row_index = jnp.arange(PXU, dtype=jnp.int32)
    rim_index = jnp.arange(3 * PXU, dtype=jnp.int32)
    spread = rim_index[None, :] - PXU - row_index[:, None]
    inside = (jnp.abs(spread) <= PXU).astype(jnp.float32)
    return along_weight(spread.astype(jnp.float32)) * inside / norm_total


def cross_matrix(count):
    point_index = jnp.arange(count, dtype=jnp.int32)
    offset = (point_index[:, None] - point_index[None, :]).astype(jnp.float32)
    kept = jnp.exp(-offset * offset / (2.0 * cross_sigma * cross_sigma)) * (
        jnp.abs(offset) <= cross_reach
    ).astype(jnp.float32)
    return kept / jnp.sum(kept, axis=1, keepdims=True)


def on_device(
    forward_displacement,
    forward_velocity,
    adjoint_displacement,
    adjoint_velocity,
    inverse_mass,
    shear_modulus,
    connectivity,
    face_points,
    element_count,
):
    derivative, weights_cube = gll_tables()
    faces = face_points[0]
    elements = connectivity.shape[1]
    active = (jnp.arange(elements, dtype=jnp.int32) < element_count[0]).astype(jnp.float32)
    flux = weights_cube[:, None] * shear_modulus * active[None, :]
    flux_cube = flux.reshape(NGLL, NGLL, NGLL, elements)
    forward_now = forward_displacement[0]
    adjoint_now = adjoint_displacement[0]
    both_now = jnp.stack([forward_now, adjoint_now])
    both_ghost = from_behind(both_now[:, faces], "cuts", -1)
    both_ext = jnp.concatenate([both_now, both_ghost], axis=1)
    gathered = both_ext[:, connectivity]
    cubes = gathered.transpose(1, 0, 2).reshape(NGLL, NGLL, NGLL, 2 * elements)
    both_grads = gradients(cubes, derivative)
    both_flux = jnp.concatenate([flux_cube, flux_cube], axis=3)
    both_force = stiffness(both_grads, both_flux, derivative)
    forward_term = both_force[..., :elements]
    adjoint_term = both_force[..., elements:]
    product = (
        both_grads[0][..., :elements] * both_grads[0][..., elements:]
        + both_grads[1][..., :elements] * both_grads[1][..., elements:]
        + both_grads[2][..., :elements] * both_grads[2][..., elements:]
    )
    kernel_term = -flux_cube * product
    stacked_terms = jnp.stack(
        [forward_term.reshape(-1), adjoint_term.reshape(-1), kernel_term.reshape(-1)], axis=1
    )
    point_ids = connectivity.reshape(-1)
    total = NPTS + NBUF
    summed_terms = jax.ops.segment_sum(stacked_terms, point_ids, num_segments=total)
    forward_force = summed_terms[:, 0]
    adjoint_force = summed_terms[:, 1]
    kernel_ext = summed_terms[:, 2]
    back_forward, back_adjoint, back_kernel = from_behind(
        (forward_force[NPTS:], adjoint_force[NPTS:], kernel_ext[NPTS:]), "cuts", 1
    )
    forward_force = forward_force[:NPTS].at[faces].add(back_forward)
    adjoint_force = adjoint_force[:NPTS].at[faces].add(back_adjoint)
    kernel_points = kernel_ext[:NPTS].at[faces].add(back_kernel)
    forward_speed_next = forward_velocity[0] - time_step * inverse_mass * forward_force
    forward_now_next = forward_now - time_step * forward_speed_next
    adjoint_speed_next = adjoint_velocity[0] + time_step * inverse_mass * adjoint_force
    adjoint_now_next = adjoint_now + time_step * adjoint_speed_next
    event_kernel = kernel_points.reshape(PXU, PYZ)
    band = along_band()
    cross = jnp.kron(cross_matrix(PY), cross_matrix(PZ))
    summed = lax.psum(event_kernel, "event")
    rimmed = with_halo(summed, (("cuts", 0),), PXU)
    smoothed_along = jnp.dot(band, rimmed, precision=lax.Precision.HIGHEST)
    shear_kernel = jnp.dot(smoothed_along, cross.T, precision=lax.Precision.HIGHEST)
    return (
        forward_now_next[None, :],
        forward_speed_next[None, :],
        adjoint_now_next[None, :],
        adjoint_speed_next[None, :],
        shear_kernel,
    )


def solution(mesh):
    in_specs = (
        P("event", "cuts"),
        P("event", "cuts"),
        P("event", "cuts"),
        P("event", "cuts"),
        P("cuts"),
        P(None, "cuts"),
        P(None, "cuts"),
        P("cuts", None),
        P("cuts"),
    )
    out_specs = (
        P("event", "cuts"),
        P("event", "cuts"),
        P("event", "cuts"),
        P("event", "cuts"),
        P("cuts", None),
    )
    return jax.shard_map(
        on_device, mesh=mesh, in_specs=in_specs, out_specs=out_specs, check_vma=False
    )
```

profile of v0, /device:TPU:121, one launch (start us, length us, event | category | flops | bytes accessed | tf_op | source)
XLA Modules:
  0.0 436.7 jit_solution(18053370572969491955)
XLA Ops:
  7.2 0.7 fusion.35
  8.0 1.1 pad_maximum_fusion.2
  9.1 5.1 %copy.95 = f32[2,17424]{0,1:T(8,128)} copy(f32[2,17424]{1,0:T(2,128)S(1)} %pad_maximum_fusion.2) | data formatting | bytes 278784 | tf_op jit(solution)/shard_map/stack | solution.py:139
  14.1 6.0 %gather_fusion = f32[1152,2]{1,0:T(8,128)S(1)} fusion(f32[2,17424]{0,1:T(8,128)} %copy.95, s32[2048]{0:T(1024)S(1)} %pad_clamp_fusion.1), kind=kCustom, calls=%fused_computation | custom fusion | bytes 23040 | tf_op jit(solution)/shard_map/gather | solution.py:140
  22.1 8.9 %broadcast_multiply_fusion = f32[33,33,33,33]{3,2,1,0:T(8,128)} fusion(f32[33,33]{1,0:T(8,128)S(1)} %fusion.25), kind=kLoop, calls=%fused_computation.6 | loop fusion | flops 1185921 | bytes 4748040 | tf_op jit(solution)/shard_map/jit(kron)/mul | solution.py:176
  31.3 5.3 %copy.97 = f32[2,18576]{0,1:T(8,128)} copy(f32[2,18576]{1,0:T(2,128)S(1)} %pad_maximum_fusion.1) | data formatting | bytes 297216 | tf_op jit(solution)/shard_map/concatenate | solution.py:141
  36.6 63.0 %gather_fusion.1 = f32[32000,2]{1,0:T(8,128)} fusion(f32[2,18576]{0,1:T(8,128)} %copy.97, s32[32768]{0:T(1024)S(1)} %pad_clamp_fusion), kind=kCustom, calls=%fused_computation.1 | custom fusion | bytes 640000 | tf_op jit(solution)/shard_map/gather | solution.py:142
  99.5 9.1 %copy.98 = f32[125,2,256]{2,1,0:T(2,128)S(1)} copy(f32[125,2,256]{1,2,0:T(8,128)} %bitcast.37) | data formatting | bytes 512000 | tf_op jit(solution)/shard_map/transpose | solution.py:143
  112.7 0.8 fusion.3
  114.5 8.5 %copy.114 = f32[32000,3]{1,0:T(8,128)} copy(f32[32000,3]{0,1:T(4,128)S(1)} %pad_maximum_fusion) | data formatting | bytes 768000 | tf_op jit(solution)/shard_map/stack | solution.py:155
  123.0 176.6 %scatter_custom_fusion = f32[18576,3]{1,0:T(8,128)} fusion(s32[32000]{0:T(1024)S(1)} %reshape.155, f32[32000,3]{1,0:T(8,128)} %copy.114, f32[]{:T(128)} %constant.13.clone.1), kind=kCustom, calls=%fused_computation.10 | custom fusion | flops 96000 | bytes 223424 | tf_op jit(solution)/shard_map/scatter-add | solution.py:160
  299.7 2.5 slice_reduce_fusion.3
  302.1 5.4 %collective-permute-start.3 = (f32[1152]{0:T(1024)S(1)}, f32[1152]{0:T(1024)S(1)}, u32[]{:S(2)}, u32[]{:S(2)}) collective-permute-start(f32[1152]{0:T(1024)S(1)} %get-tuple-element.5), channel_id=1, source_target_pairs={{31,0},{0,1},{1,2},{2,3},{3,4},{4,5},{5,6},{6,7},{7,8},{8,9},{9,10... | collective-permute-start | bytes 13832 | tf_op jit(solution)/shard_map/ppermute | solution.py:22
  307.5 16.4 %slice_reduce_fusion = (f32[17424]{0:T(1024)S(1)}, f32[17424]{0:T(1024)S(1)}, f32[17424]{0:T(1024)S(1)}) fusion(f32[18576,3]{1,0:T(8,128)} %scatter_custom_fusion), kind=kLoop, calls=%fused_computation.7 | loop fusion | bytes 418176 | tf_op jit(solution)/shard_map/slice | solution.py:169
  324.1 8.8 %scatter_fusion.2 = f32[17424]{0:T(1024)S(1)} fusion(f32[17424]{0:T(1024)S(1)} %get-tuple-element.8, s32[1152]{0:T(1024)S(1)} %fusion.35, f32[1152]{0:T(1024)S(1)} %collective-permute-done.3), kind=kCustom, calls=%fused_computation.5 | custom fusion | flops 1152 | bytes 18432 | tf_op jit(solution)/shard_map/scatter-add | solution.py:169
  332.9 0.7 reshape.136
  334.1 15.5 %mul.130 = f32[1089,1089]{1,0:T(8,128)} reshape(f32[33,33,33,33]{3,2,1,0:T(8,128)} %broadcast_multiply_fusion) | data formatting | bytes 9487368 | tf_op jit(solution)/shard_map/jit(kron)/mul | solution.py:176
  350.7 8.8 %scatter_fusion = f32[17424]{0:T(1024)S(1)} fusion(f32[17424]{0:T(1024)S(1)} %get-tuple-element.10, s32[1152]{0:T(1024)S(1)} %fusion.35, f32[1152]{0:T(1024)S(1)} %collective-permute-done.1), kind=kCustom, calls=%fused_computation.3 | custom fusion | flops 1152 | bytes 18432 | tf_op jit(solution)/shard_map/scatter-add | solution.py:167
  359.5 9.0 %scatter_fusion.1 = f32[17424]{0:T(1024)S(1)} fusion(f32[17424]{0:T(1024)S(1)} %get-tuple-element.9, s32[1152]{0:T(1024)S(1)} %fusion.35, f32[1152]{0:T(1024)S(1)} %collective-permute-done.2), kind=kCustom, calls=%fused_computation.4 | custom fusion | flops 1152 | bytes 18432 | tf_op jit(solution)/shard_map/scatter-add | solution.py:168
  368.6 35.2 %all-reduce.2.cloned.1.call-done = f32[16,1089]{1,0:T(8,128)} async-done(((f32[16,1089]{1,0:T(8,128)}), f32[16,1089]{1,0:T(8,128)}) %all-reduce.2.cloned.1.call-update) | async-done | bytes 69712 | tf_op jit(solution)/shard_map/psum | solution.py:177
  403.7 8.9 %collective-permute-start.4 = (f32[16,1089]{1,0:T(8,128)}, f32[16,1089]{1,0:T(8,128)S(1)}, u32[]{:S(2)}, u32[]{:S(2)}) collective-permute-start(f32[16,1089]{1,0:T(8,128)} %all-reduce.2.cloned.1.call-done), channel_id=1, source_target_pairs={{0,1},{1,2},{2,3},{3,4},{4,5},{5,6},{6,7},{7,8},{8,9},{9,10},{10,1... | collective-permute-start | bytes 209096 | tf_op jit(solution)/shard_map/ppermute | solution.py:32
  415.4 5.4 %collective-permute-done.5 = f32[16,1089]{1,0:T(8,128)S(1)} collective-permute-done((f32[16,1089]{1,0:T(8,128)}, f32[16,1089]{1,0:T(8,128)S(1)}, u32[]{:S(2)}, u32[]{:S(2)}) %collective-permute-start.5) | collective-permute-done | bytes 69728 | tf_op jit(solution)/shard_map/ppermute | solution.py:34
  420.8 1.8 fusion.13
  422.6 7.3 %fusion.52 = f32[16,1089]{1,0:T(8,128)} fusion(f32[16,1089]{1,0:T(8,128)S(1)} %fusion.13, f32[1089,1089]{1,0:T(8,128)} %mul.130), kind=kOutput, calls=%fused_computation.91 | convolution fusion | flops 227696832 | bytes 4883076 | tf_op jit(solution)/shard_map/dot_general | solution.py:180
  (71 shorter events, 10.9 us)
Async XLA Ops:
  7.2 14.7 %copy-start.8 = (f32[125]{0:T(128)S(1)}, f32[125]{0:T(128)}, u32[]{:S(2)}) copy-start(f32[125]{0:T(128)} %constant.35.clone) | copy-start | bytes 1504
  7.2 14.0 %copy-start.2 = (s32[125,256]{1,0:T(8,128)S(1)}, s32[125,256]{1,0:T(8,128)}, u32[]{:S(2)}) copy-start(s32[125,256]{1,0:T(8,128)} %param.17) | copy-start | bytes 384004
  7.2 14.7 %copy-start.4 = (f32[125,256]{1,0:T(8,128)S(1)}, f32[125,256]{1,0:T(8,128)}, u32[]{:S(2)}) copy-start(f32[125,256]{1,0:T(8,128)} %param.16) | copy-start | bytes 384004
  7.2 396.5 %all-reduce.2.cloned.1.call-start = ((), (), s32[]{:S(2)}) async-start(), calls=%async_computation | async-start | bytes 147456 | tf_op jit(solution)/shard_map/psum | solution.py:177
  20.3 10.8 %collective-permute-start = (f32[2,1152]{1,0:T(2,128)S(1)}, f32[2,1152]{1,0:T(2,128)S(1)}, u32[]{:S(2)}, u32[]{:S(2)}) collective-permute-start(f32[2,1152]{1,0:T(2,128)S(1)} %copy.96), channel_id=1, source_target_pairs={{1,0},{2,1},{3,2},{4,3},{5,4},{6,5},{7,6},{8,7},{9,8},{10,9},{11,1... | collective-permute-start | bytes 27656 | tf_op jit(solution)/shard_map/ppermute | solution.py:22
  22.1 9.0 %copy-start = (f32[1,17424]{1,0:T(1,128)S(1)}, f32[1,17424]{1,0:T(1,128)}, u32[]{:S(2)}) copy-start(f32[1,17424]{1,0:T(1,128)} %param.11) | copy-start | bytes 209092
  22.1 9.0 %copy-start.1 = (f32[1,17424]{1,0:T(1,128)S(1)}, f32[1,17424]{1,0:T(1,128)}, u32[]{:S(2)}) copy-start(f32[1,17424]{1,0:T(1,128)} %param.13) | copy-start | bytes 209092
  36.6 72.3 %copy-start.3 = (f32[5,5,1,1]{1,0,3,2:T(8,128)S(1)}, f32[5,5,1,1]{1,0,3,2:T(8,128)}, u32[]{:S(2)}) copy-start(f32[5,5,1,1]{1,0,3,2:T(8,128)} %constant.43) | copy-start | bytes 304
  302.1 22.0 %collective-permute-start.3 = (f32[1152]{0:T(1024)S(1)}, f32[1152]{0:T(1024)S(1)}, u32[]{:S(2)}, u32[]{:S(2)}) collective-permute-start(f32[1152]{0:T(1024)S(1)} %get-tuple-element.5), channel_id=1, source_target_pairs={{31,0},{0,1},{1,2},{2,3},{3,4},{4,5},{5,6},{6,7},{7,8},{8,9},{9,10... | collective-permute-start | bytes 13832 | tf_op jit(solution)/shard_map/ppermute | solution.py:22
  323.9 26.8 %collective-permute-start.1 = (f32[1152]{0:T(1024)S(1)}, f32[1152]{0:T(1024)S(1)}, u32[]{:S(2)}, u32[]{:S(2)}) collective-permute-start(f32[1152]{0:T(1024)S(1)} %get-tuple-element.7), channel_id=1, source_target_pairs={{31,0},{0,1},{1,2},{2,3},{3,4},{4,5},{5,6},{6,7},{7,8},{8,9},{9,10... | collective-permute-start | bytes 13832 | tf_op jit(solution)/shard_map/ppermute | solution.py:22
  324.0 35.5 %collective-permute-start.2 = (f32[1152]{0:T(1024)S(1)}, f32[1152]{0:T(1024)S(1)}, u32[]{:S(2)}, u32[]{:S(2)}) collective-permute-start(f32[1152]{0:T(1024)S(1)} %get-tuple-element.6), channel_id=1, source_target_pairs={{31,0},{0,1},{1,2},{2,3},{3,4},{4,5},{5,6},{6,7},{7,8},{8,9},{9,10... | collective-permute-start | bytes 13832 | tf_op jit(solution)/shard_map/ppermute | solution.py:22
  334.0 15.6 %copy-start.6 = (f32[1,17424]{1,0:T(1,128)S(1)}, f32[1,17424]{1,0:T(1,128)}, u32[]{:S(2)}) copy-start(f32[1,17424]{1,0:T(1,128)} %param.12) | copy-start | bytes 209092
  334.1 15.7 %copy-start.7 = (f32[1,17424]{1,0:T(1,128)S(1)}, f32[1,17424]{1,0:T(1,128)}, u32[]{:S(2)}) copy-start(f32[1,17424]{1,0:T(1,128)} %param.14) | copy-start | bytes 209092
  359.5 53.1 %copy-start.5 = (f32[17424]{0:T(1024)S(1)}, f32[17424]{0:T(1024)}, u32[]{:S(2)}) copy-start(f32[17424]{0:T(1024)} %param.15) | copy-start | bytes 209092
  403.7 11.7 %collective-permute-start.4 = (f32[16,1089]{1,0:T(8,128)}, f32[16,1089]{1,0:T(8,128)S(1)}, u32[]{:S(2)}, u32[]{:S(2)}) collective-permute-start(f32[16,1089]{1,0:T(8,128)} %all-reduce.2.cloned.1.call-done), channel_id=1, source_target_pairs={{0,1},{1,2},{2,3},{3,4},{4,5},{5,6},{6,7},{7,8},{8,9},{9,10},{10,1... | collective-permute-start | bytes 209096 | tf_op jit(solution)/shard_map/ppermute | solution.py:32
  412.6 8.2 %collective-permute-start.5 = (f32[16,1089]{1,0:T(8,128)}, f32[16,1089]{1,0:T(8,128)S(1)}, u32[]{:S(2)}, u32[]{:S(2)}) collective-permute-start(f32[16,1089]{1,0:T(8,128)} %all-reduce.2.cloned.1.call-done), channel_id=1, source_target_pairs={{1,0},{2,1},{3,2},{4,3},{5,4},{6,5},{7,6},{8,7},{9,8},{10,9},{11,1... | collective-permute-start | bytes 209096 | tf_op jit(solution)/shard_map/ppermute | solution.py:34
Sparse Core Ops, SparseCore 0:
  333.8 69.8 all-reduce.1
where the time goes:
time: 437 us
  other arithmetic  217 us (50%)
  local copies, waits for them, and re-layouts  136 us (31%)
  waiting for transfers between devices  40.6 us (9%)
  starting transfers between devices  15.2 us (3%)
  between operations  15.1 us (3%)
  matrix products  12.8 us (3%)
    scatter-add x1, other arithmetic, on_device(): jax.ops.segment_sum(stacked_terms, point_ids, num_segments=total)  177 us
    gather x1, local copies, waits for them, and re-layouts, on_device(): gathered = both_ext[:, connectivity]  63 us
    psum x1, waiting for transfers between devices, on_device(): summed = lax.psum(event_kernel, 'event')  35.2 us
    slice x1, local copies, waits for them, and re-layouts, on_device(): kernel_points = kernel_ext[:NPTS].at[faces].add(back_kernel)  16.4 us
    mul x1, local copies, waits for them, and re-layouts, on_device(): cross = jnp.kron(cross_matrix(PY), cross_matrix(PZ))  15.5 us
    transpose x1, local copies, waits for them, and re-layouts, on_device(): cubes = gathered.transpose(1, 0, 2).reshape(NGLL, NGLL, NGLL, 2 * elements)  9.08 us
    scatter-add x1, other arithmetic, on_device(): adjoint_force = adjoint_force[:NPTS].at[faces].add(back_adjoint)  9.04 us
    mul x1, other arithmetic, on_device(): cross = jnp.kron(cross_matrix(PY), cross_matrix(PZ))  8.92 us
  transfers between devices with their start and end apart: 7, of which 2 were waited for; matrix products, arithmetic and copies ran while one was open for 17% of the time, Pallas kernels for 0%

commit v1 on v0

--- a/solution.py
+++ b/solution.py
@@ -174,7 +174,7 @@
     event_kernel = kernel_points.reshape(PXU, PYZ)
     band = along_band()
     cross = jnp.kron(cross_matrix(PY), cross_matrix(PZ))
-    summed = lax.psum(event_kernel, "event")
+    summed = jnp.sum(lax.all_gather(event_kernel, "event"), axis=0)
     rimmed = with_halo(summed, (("cuts", 0),), PXU)
     smoothed_along = jnp.dot(band, rimmed, precision=lax.Precision.HIGHEST)
     shear_kernel = jnp.dot(smoothed_along, cross.T, precision=lax.Precision.HIGHEST)

time: 437 us -> 410 us (0.938); the launches traced: 437 us -> 403 us
  waiting for transfers between devices: 40.6 us -> 0.02 us
  blocking collectives: 0 us -> 24.5 us
  between operations: 15.1 us -> 1.72 us
    psum x1 -> x0, waiting for transfers between devices: 35.2 us -> none  [on_device(): summed = lax.psum(event_kernel, 'event')]
    all_gather x0 -> x1, blocking collectives: none -> 24.5 us  [on_device(): summed = jnp.sum(lax.all_gather(event_kernel, 'event'), axis=0)]
    ppermute x1, waiting for transfers between devices: 5.44 us -> 0.01 us  [with_halo(): lax.ppermute(head, axis, [((i + 1) % count, i) for i in range(count)])]
  transfers between devices with their start and end apart: 7 -> 6, of which waited for: 2 -> 0; matrix products, arithmetic and copies ran while one was open for 17% -> 18% of each run, Pallas kernels for 0% -> 0%
where the time goes in v1:
time: 410 us; the launch traced here: 403 us
  other arithmetic  217 us (53%)
  local copies, waits for them, and re-layouts  135 us (33%)
  blocking collectives  24.5 us (6%)
  starting transfers between devices  12.7 us (3%)
  matrix products  11.9 us (3%)
    scatter-add x1, other arithmetic, on_device(): jax.ops.segment_sum(stacked_terms, point_ids, num_segments=total)  177 us
    gather x1, local copies, waits for them, and re-layouts, on_device(): gathered = both_ext[:, connectivity]  62.8 us
    all_gather x1, blocking collectives, on_device(): summed = jnp.sum(lax.all_gather(event_kernel, 'event'), axis=0)  24.5 us
    slice x1, local copies, waits for them, and re-layouts, on_device(): kernel_points = kernel_ext[:NPTS].at[faces].add(back_kernel)  16.4 us
    mul x1, local copies, waits for them, and re-layouts, on_device(): cross = jnp.kron(cross_matrix(PY), cross_matrix(PZ))  15.6 us
    transpose x1, local copies, waits for them, and re-layouts, on_device(): cubes = gathered.transpose(1, 0, 2).reshape(NGLL, NGLL, NGLL, 2 * elements)  9.08 us
    scatter-add x1, other arithmetic, on_device(): adjoint_force = adjoint_force[:NPTS].at[faces].add(back_adjoint)  9.04 us
    mul x1, other arithmetic, on_device(): cross = jnp.kron(cross_matrix(PY), cross_matrix(PZ))  8.92 us
  transfers between devices with their start and end apart: 6, of which 0 were waited for; matrix products, arithmetic and copies ran while one was open for 18% of the time, Pallas kernels for 0%

profile of v1, /device:TPU:121, one launch (start us, length us, event | category | flops | bytes accessed | tf_op | source)
XLA Modules:
  0.0 402.8 jit_solution(6645985841159260579)
XLA Ops:
  0.7 0.8 fusion.35
  1.4 1.1 pad_maximum_fusion.2
  2.5 5.1 %copy.95 = f32[2,17424]{0,1:T(8,128)} copy(f32[2,17424]{1,0:T(2,128)S(1)} %pad_maximum_fusion.2) | data formatting | bytes 278784 | tf_op jit(solution)/shard_map/stack | solution.py:139
  7.5 6.0 %gather_fusion = f32[1152,2]{1,0:T(8,128)S(1)} fusion(f32[2,17424]{0,1:T(8,128)} %copy.95, s32[2048]{0:T(1024)S(1)} %pad_clamp_fusion.1), kind=kCustom, calls=%fused_computation | custom fusion | bytes 23040 | tf_op jit(solution)/shard_map/gather | solution.py:140
  13.7 0.7 collective-permute-start
  15.6 8.9 %broadcast_multiply_fusion = f32[33,33,33,33]{3,2,1,0:T(8,128)} fusion(f32[33,33]{1,0:T(8,128)S(1)} %fusion.25), kind=kLoop, calls=%fused_computation.6 | loop fusion | flops 1185921 | bytes 4748040 | tf_op jit(solution)/shard_map/jit(kron)/mul | solution.py:176
  24.9 15.6 %mul.130 = f32[1089,1089]{1,0:T(8,128)} reshape(f32[33,33,33,33]{3,2,1,0:T(8,128)} %broadcast_multiply_fusion) | data formatting | bytes 9487368 | tf_op jit(solution)/shard_map/jit(kron)/mul | solution.py:176
  41.6 5.3 %copy.97 = f32[2,18576]{0,1:T(8,128)} copy(f32[2,18576]{1,0:T(2,128)S(1)} %pad_maximum_fusion.1) | data formatting | bytes 297216 | tf_op jit(solution)/shard_map/concatenate | solution.py:141
  46.9 62.8 %gather_fusion.1 = f32[32000,2]{1,0:T(8,128)} fusion(f32[2,18576]{0,1:T(8,128)} %copy.97, s32[32768]{0:T(1024)S(1)} %pad_clamp_fusion), kind=kCustom, calls=%fused_computation.1 | custom fusion | bytes 640000 | tf_op jit(solution)/shard_map/gather | solution.py:142
  109.8 9.1 %copy.98 = f32[125,2,256]{2,1,0:T(2,128)S(1)} copy(f32[125,2,256]{1,2,0:T(8,128)} %bitcast.37) | data formatting | bytes 512000 | tf_op jit(solution)/shard_map/transpose | solution.py:143
  122.9 0.8 fusion.3
  124.7 8.4 %copy.114 = f32[32000,3]{1,0:T(8,128)} copy(f32[32000,3]{0,1:T(4,128)S(1)} %pad_maximum_fusion) | data formatting | bytes 768000 | tf_op jit(solution)/shard_map/stack | solution.py:155
  133.2 176.6 %scatter_custom_fusion = f32[18576,3]{1,0:T(8,128)} fusion(s32[32000]{0:T(1024)S(1)} %reshape.151, f32[32000,3]{1,0:T(8,128)} %copy.114, f32[]{:T(128)} %constant.13.clone.1), kind=kCustom, calls=%fused_computation.10 | custom fusion | flops 96000 | bytes 223424 | tf_op jit(solution)/shard_map/scatter-add | solution.py:160
  309.7 2.4 slice_reduce_fusion.3
  312.1 5.4 %collective-permute-start.3 = (f32[1152]{0:T(1024)S(1)}, f32[1152]{0:T(1024)S(1)}, u32[]{:S(2)}, u32[]{:S(2)}) collective-permute-start(f32[1152]{0:T(1024)S(1)} %get-tuple-element.5), channel_id=1, source_target_pairs={{31,0},{0,1},{1,2},{2,3},{3,4},{4,5},{5,6},{6,7},{7,8},{8,9},{9,10... | collective-permute-start | bytes 13832 | tf_op jit(solution)/shard_map/ppermute | solution.py:22
  317.5 16.4 %slice_reduce_fusion = (f32[17424]{0:T(1024)S(1)}, f32[17424]{0:T(1024)S(1)}, f32[17424]{0:T(1024)S(1)}) fusion(f32[18576,3]{1,0:T(8,128)} %scatter_custom_fusion), kind=kLoop, calls=%fused_computation.7 | loop fusion | bytes 418176 | tf_op jit(solution)/shard_map/slice | solution.py:169
  334.1 8.8 %scatter_fusion.2 = f32[17424]{0:T(1024)S(1)} fusion(f32[17424]{0:T(1024)S(1)} %get-tuple-element.8, s32[1152]{0:T(1024)S(1)} %fusion.35, f32[1152]{0:T(1024)S(1)} %collective-permute-done.3), kind=kCustom, calls=%fused_computation.5 | custom fusion | flops 1152 | bytes 18432 | tf_op jit(solution)/shard_map/scatter-add | solution.py:169
  343.1 24.5 %all_gather.3 = f32[8,16,1089]{2,1,0:T(8,128)S(1)} all-gather(f32[1,16,1089]{2,1,0:T(8,128)S(1)} %all_gather_reshape.3), channel_id=1, replica_groups=mesh['event'=8,'cuts'=32] {'event'}, dimensions={0}, use_global_device_ids=true | all-gather | bytes 627264 | tf_op jit(solution)/shard_map/all_gather | solution.py:177
  367.6 6.1 %collective-permute-start.4 = (f32[16,1089]{1,0:T(8,128)S(1)}, f32[16,1089]{1,0:T(8,128)S(1)}, u32[]{:S(2)}, u32[]{:S(2)}) collective-permute-start(f32[16,1089]{1,0:T(8,128)S(1)} %reduce_sum.32), channel_id=1, source_target_pairs={{0,1},{1,2},{2,3},{3,4},{4,5},{5,6},{6,7},{7,8},{8,9},{9,10},{10,1... | collective-permute-start | bytes 209096 | tf_op jit(solution)/shard_map/ppermute | solution.py:32
  374.0 8.8 %scatter_fusion = f32[17424]{0:T(1024)S(1)} fusion(f32[17424]{0:T(1024)S(1)} %get-tuple-element.10, s32[1152]{0:T(1024)S(1)} %fusion.35, f32[1152]{0:T(1024)S(1)} %collective-permute-done.1), kind=kCustom, calls=%fused_computation.3 | custom fusion | flops 1152 | bytes 18432 | tf_op jit(solution)/shard_map/scatter-add | solution.py:167
  382.8 9.0 %scatter_fusion.1 = f32[17424]{0:T(1024)S(1)} fusion(f32[17424]{0:T(1024)S(1)} %get-tuple-element.9, s32[1152]{0:T(1024)S(1)} %fusion.35, f32[1152]{0:T(1024)S(1)} %collective-permute-done.2), kind=kCustom, calls=%fused_computation.4 | custom fusion | flops 1152 | bytes 18432 | tf_op jit(solution)/shard_map/scatter-add | solution.py:168
  391.9 0.7 broadcast_in_dim.16
  394.7 0.9 fusion.13
  395.6 7.3 %fusion.52 = f32[16,1089]{1,0:T(8,128)} fusion(f32[16,1089]{1,0:T(8,128)S(1)} %fusion.13, f32[1089,1089]{1,0:T(8,128)} %mul.130), kind=kOutput, calls=%fused_computation.91 | convolution fusion | flops 227696832 | bytes 4883076 | tf_op jit(solution)/shard_map/dot_general | solution.py:180
  (70 shorter events, 9.7 us)
Async XLA Ops:
  0.6 14.7 %copy-start.8 = (f32[125]{0:T(128)S(1)}, f32[125]{0:T(128)}, u32[]{:S(2)}) copy-start(f32[125]{0:T(128)} %constant.35.clone) | copy-start | bytes 1504
  0.6 13.9 %copy-start.2 = (s32[125,256]{1,0:T(8,128)S(1)}, s32[125,256]{1,0:T(8,128)}, u32[]{:S(2)}) copy-start(s32[125,256]{1,0:T(8,128)} %param.17) | copy-start | bytes 384004
  0.7 14.6 %copy-start.4 = (f32[125,256]{1,0:T(8,128)S(1)}, f32[125,256]{1,0:T(8,128)}, u32[]{:S(2)}) copy-start(f32[125,256]{1,0:T(8,128)} %param.16) | copy-start | bytes 384004
  13.7 27.8 %collective-permute-start = (f32[2,1152]{1,0:T(2,128)S(1)}, f32[2,1152]{1,0:T(2,128)S(1)}, u32[]{:S(2)}, u32[]{:S(2)}) collective-permute-start(f32[2,1152]{1,0:T(2,128)S(1)} %copy.96), channel_id=1, source_target_pairs={{1,0},{2,1},{3,2},{4,3},{5,4},{6,5},{7,6},{8,7},{9,8},{10,9},{11,1... | collective-permute-start | bytes 27656 | tf_op jit(solution)/shard_map/ppermute | solution.py:22
  15.6 9.0 %copy-start.1 = (f32[1,17424]{1,0:T(1,128)S(1)}, f32[1,17424]{1,0:T(1,128)}, u32[]{:S(2)}) copy-start(f32[1,17424]{1,0:T(1,128)} %param.11) | copy-start | bytes 209092
  15.6 9.1 %copy-start = (f32[1,17424]{1,0:T(1,128)S(1)}, f32[1,17424]{1,0:T(1,128)}, u32[]{:S(2)}) copy-start(f32[1,17424]{1,0:T(1,128)} %param.13) | copy-start | bytes 209092
  24.9 15.6 %copy-start.6 = (f32[1,17424]{1,0:T(1,128)S(1)}, f32[1,17424]{1,0:T(1,128)}, u32[]{:S(2)}) copy-start(f32[1,17424]{1,0:T(1,128)} %param.12) | copy-start | bytes 209092
  24.9 15.8 %copy-start.7 = (f32[1,17424]{1,0:T(1,128)S(1)}, f32[1,17424]{1,0:T(1,128)}, u32[]{:S(2)}) copy-start(f32[1,17424]{1,0:T(1,128)} %param.14) | copy-start | bytes 209092
  46.9 72.1 %copy-start.3 = (f32[5,5,1,1]{1,0,3,2:T(8,128)S(1)}, f32[5,5,1,1]{1,0,3,2:T(8,128)}, u32[]{:S(2)}) copy-start(f32[5,5,1,1]{1,0,3,2:T(8,128)} %constant.43) | copy-start | bytes 304
  312.1 22.0 %collective-permute-start.3 = (f32[1152]{0:T(1024)S(1)}, f32[1152]{0:T(1024)S(1)}, u32[]{:S(2)}, u32[]{:S(2)}) collective-permute-start(f32[1152]{0:T(1024)S(1)} %get-tuple-element.5), channel_id=1, source_target_pairs={{31,0},{0,1},{1,2},{2,3},{3,4},{4,5},{5,6},{6,7},{7,8},{8,9},{9,10... | collective-permute-start | bytes 13832 | tf_op jit(solution)/shard_map/ppermute | solution.py:22
  333.9 40.1 %collective-permute-start.1 = (f32[1152]{0:T(1024)S(1)}, f32[1152]{0:T(1024)S(1)}, u32[]{:S(2)}, u32[]{:S(2)}) collective-permute-start(f32[1152]{0:T(1024)S(1)} %get-tuple-element.7), channel_id=1, source_target_pairs={{31,0},{0,1},{1,2},{2,3},{3,4},{4,5},{5,6},{6,7},{7,8},{8,9},{9,10... | collective-permute-start | bytes 13832 | tf_op jit(solution)/shard_map/ppermute | solution.py:22
  334.0 48.8 %collective-permute-start.2 = (f32[1152]{0:T(1024)S(1)}, f32[1152]{0:T(1024)S(1)}, u32[]{:S(2)}, u32[]{:S(2)}) collective-permute-start(f32[1152]{0:T(1024)S(1)} %get-tuple-element.6), channel_id=1, source_target_pairs={{31,0},{0,1},{1,2},{2,3},{3,4},{4,5},{5,6},{6,7},{7,8},{8,9},{9,10... | collective-permute-start | bytes 13832 | tf_op jit(solution)/shard_map/ppermute | solution.py:22
  367.6 27.0 %collective-permute-start.4 = (f32[16,1089]{1,0:T(8,128)S(1)}, f32[16,1089]{1,0:T(8,128)S(1)}, u32[]{:S(2)}, u32[]{:S(2)}) collective-permute-start(f32[16,1089]{1,0:T(8,128)S(1)} %reduce_sum.32), channel_id=1, source_target_pairs={{0,1},{1,2},{2,3},{3,4},{4,5},{5,6},{6,7},{7,8},{8,9},{9,10},{10,1... | collective-permute-start | bytes 209096 | tf_op jit(solution)/shard_map/ppermute | solution.py:32
  373.7 20.9 %collective-permute-start.5 = (f32[16,1089]{1,0:T(8,128)S(1)}, f32[16,1089]{1,0:T(8,128)S(1)}, u32[]{:S(2)}, u32[]{:S(2)}) collective-permute-start(f32[16,1089]{1,0:T(8,128)S(1)} %reduce_sum.32), channel_id=1, source_target_pairs={{1,0},{2,1},{3,2},{4,3},{5,4},{6,5},{7,6},{8,7},{9,8},{10,9},{11,1... | collective-permute-start | bytes 209096 | tf_op jit(solution)/shard_map/ppermute | solution.py:34
  382.8 9.1 %copy-start.5 = (f32[17424]{0:T(1024)S(1)}, f32[17424]{0:T(1024)}, u32[]{:S(2)}) copy-start(f32[17424]{0:T(1024)} %param.15) | copy-start | bytes 209092
